TPU v7x, 32 devices: a whole 2x2x4 slice. The times are simulated.
32 devices in a mesh: heads: 4 (over x, core), seq: 8 (over z, y).
Axes of the slice: x: 2, y: 2, z: 4, core: 2. Of those that a mesh axis runs over, the one named last changes fastest.
Arguments:
- tokens: bfloat16 [2048, 4096], P('seq'), may hold values from -6 to 6
- norm_gain: float32 [4096], replicated, may hold values from 0.1 to 1.9
- w_query: bfloat16 [4096, 4096], P(None, 'heads'), may hold values from -0.09375 to 0.09375
- w_key: bfloat16 [4096, 1024], P(None, 'heads'), may hold values from -0.1875 to 0.1875
- w_value: bfloat16 [4096, 1024], P(None, 'heads'), may hold values from -0.375 to 0.375
- w_out: bfloat16 [4096, 4096], P('heads'), may hold values from -0.09375 to 0.09375
- cache_keys: bfloat16 [8, 8192, 128], P('heads', 'seq'), may hold values from -360 to 360
- cache_values: bfloat16 [8, 8192, 128], P('heads', 'seq'), may hold values from -24 to 24
- vert_blocks: int32 [8, 64], P('heads'), may hold values from -1 to 127, as said below
- vert_count: int32 [8], P('heads'), may hold values from 32 to 64
- slash_offsets: int32 [8, 4], P('heads'), may hold values from -1 to 4, as said below
- slash_count: int32 [8], P('heads'), may hold values from 1 to 4
Outputs:
- layer_out: bfloat16 [2048, 4096], P('seq', 'heads')
Inputs may be any that keep to these rules, and one draw needn't show every extreme that they name: `vert_blocks`: row g lists cache blocks for key/value head g: its entries before vert_count[g] are distinct, the rest are -1. The cache of one index of seq holds at most 8 of the blocks that a row lists, and exactly 8 for one index in every row. `slash_offsets`: entries of row g before slash_count[g] are distinct, the rest are -1.
All inputs are finite; a program needn't handle non-finite values.
Results may differ from a plain program's by a relative error of at most 0.015.
The roundings to bfloat16 on the way count: a program that leaves them out, or rounds other values in their place, can miss the bound.
Values may be sent and summed in bfloat16 or wider, within the bound.
A program may use at most 64 MiB of HBM per device.

v0:
```python
import math

import jax
import jax.numpy as jnp
from jax import lax
from jax.sharding import PartitionSpec as P

BLK = 64
VCAP = 8


def passed_along(block, axis, distance):
    devices = range(lax.axis_size(axis))
    route = [(i - distance, i) for i in devices if i - distance in devices]
    return lax.ppermute(block, axis, route)


def attend_slots(carried, kv_slots, slot_flags, head_queries, score_scale):
    slot_total = kv_slots.shape[0]
    block_len = kv_slots.shape[3]
    slot_group = 1
    for candidate in (32, 16, 8, 4, 2):
        slot_group = candidate
        break
    groups = slot_total // slot_group
    stacked = kv_slots.reshape((groups, slot_group) + kv_slots.shape[1:])
    grouped_flags = slot_flags.reshape(groups, slot_group, slot_flags.shape[1])

    def fold_step(running, entry):
        running_max, running_sum, accumulate = running
        kv_block, slot_ok = entry
        scores = (
            jnp.einsum(
                "krh,sknh->krsn",
                head_queries,
                kv_block[:, :, 0],
                preferred_element_type=jnp.float32,
            )
            * score_scale
        )
        scores = jnp.where(slot_ok.T[:, None, :, None], scores, -jnp.inf)
        scores = scores.reshape(scores.shape[0], scores.shape[1], -1)
        new_max = jnp.maximum(running_max, jnp.max(scores, axis=-1))
        factor = jnp.exp(running_max - new_max)
        weights = jnp.exp(scores - new_max[..., None])
        running_sum = running_sum * factor + jnp.sum(weights, axis=-1)
        rounded = weights.astype(jnp.bfloat16).reshape(
            weights.shape[0], weights.shape[1], slot_group, block_len
        )
        accumulate = accumulate * factor[..., None] + jnp.einsum(
            "krsn,sknh->krh", rounded, kv_block[:, :, 1], preferred_element_type=jnp.float32
        )
        return ((new_max, running_sum, accumulate), None)

    result, _ = lax.scan(fold_step, carried, (stacked, grouped_flags))
    return result


def local(
    tokens,
    norm_gain,
    w_query,
    w_key,
    w_value,
    w_out,
    cache_keys,
    cache_values,
    vert_blocks,
    vert_count,
    slash_offsets,
    slash_count,
):
    local_heads = cache_keys.shape[0]
    head_dim = cache_keys.shape[2]
    tok_rows = tokens.shape[0]
    group_size = w_query.shape[1] // (local_heads * head_dim)
    score_scale = 1.0 / math.sqrt(head_dim)
    seq_index = lax.axis_index("seq")
    activation = tokens.astype(jnp.float32)
    normed = (
        activation
        * lax.rsqrt(jnp.mean(activation * activation, axis=-1, keepdims=True) + 1e-05)
        * norm_gain
    ).astype(jnp.bfloat16)
    queries = jnp.dot(normed, w_query, preferred_element_type=jnp.float32).astype(jnp.bfloat16)
    key_rows = jnp.dot(normed, w_key, preferred_element_type=jnp.float32).astype(jnp.bfloat16)
    value_rows = jnp.dot(normed, w_value, preferred_element_type=jnp.float32).astype(jnp.bfloat16)
    head_queries = (
        queries.reshape(tok_rows, local_heads, group_size, head_dim)
        .transpose(1, 2, 0, 3)
        .reshape(local_heads, group_size * tok_rows, head_dim)
    )
    before_keys, before_values = passed_along((key_rows, value_rows), "seq", 1)
    prev_rows = before_keys.shape[0]
    near_keys = jnp.concatenate([before_keys, key_rows], 0).reshape(
        prev_rows + tok_rows, local_heads, head_dim
    )
    near_values = jnp.concatenate([before_values, value_rows], 0).reshape(
        prev_rows + tok_rows, local_heads, head_dim
    )
    scores = (
        jnp.einsum("krh,nkh->krn", head_queries, near_keys, preferred_element_type=jnp.float32)
        * score_scale
    )
    scores = scores.reshape(local_heads, group_size, tok_rows, prev_rows + tok_rows)
    row_index = jnp.arange(tok_rows)[:, None]
    key_index = jnp.arange(prev_rows + tok_rows)[None, :] - prev_rows
    block_gap = row_index // BLK - jnp.floor_divide(key_index, BLK)
    entries = jnp.arange(slash_offsets.shape[1])
    slash_live = entries[None, :] < slash_count[:, None]
    matched = jnp.any(
        (slash_offsets[:, :, None, None] == block_gap[None, None]) & slash_live[:, :, None, None],
        axis=1,
    )
    diagonal = (block_gap == 0) & (key_index <= row_index)
    present = seq_index * tok_rows + key_index >= 0
    allowed = (matched | diagonal[None]) & present[None]
    scores = jnp.where(allowed[:, None], scores, -jnp.inf)
    running_max = jnp.max(scores, axis=-1)
    weights = jnp.exp(scores - running_max[..., None])
    running_sum = jnp.sum(weights, axis=-1)
    accumulate = jnp.einsum(
        "kgtn,nkh->kgth",
        weights.astype(jnp.bfloat16),
        near_values,
        preferred_element_type=jnp.float32,
    )
    carried = (
        running_max.reshape(local_heads, -1),
        running_sum.reshape(local_heads, -1),
        accumulate.reshape(local_heads, -1, head_dim),
    )
    per_device = cache_keys.shape[1] // BLK
    first_block = seq_index * per_device
    cache_pairs = jnp.stack([cache_keys, cache_values], 1).reshape(
        local_heads, 2, per_device, BLK, head_dim
    )
    entry_index = jnp.arange(vert_blocks.shape[1])
    owned_here = (
        (entry_index[None, :] < vert_count[:, None])
        & (vert_blocks >= first_block)
        & (vert_blocks < first_block + per_device)
    )
    rank_slot = jnp.cumsum(owned_here.astype(jnp.int32), axis=1) - 1
    selector = (rank_slot[:, None, :] == jnp.arange(VCAP)[None, :, None]) & owned_here[:, None, :]
    slot_ids = jnp.sum(jnp.where(selector, vert_blocks[:, None, :], 0), axis=2)
    slot_live = jnp.any(selector, axis=2)
    local_index = jnp.clip(slot_ids - first_block, 0, per_device - 1)
    taken_rows = jnp.take_along_axis(cache_pairs, local_index[:, None, :, None, None], axis=2)
    taken_rows = jnp.where(
        slot_live[:, None, :, None, None], taken_rows, jnp.zeros((), taken_rows.dtype)
    )
    kv_slots = taken_rows.transpose(2, 0, 1, 3, 4)
    carried = attend_slots(
        carried,
        lax.all_gather(kv_slots, "seq", axis=0, tiled=True),
        lax.all_gather(slot_live.T.astype(jnp.int32), "seq", axis=0, tiled=True) > 0,
        head_queries,
        score_scale,
    )
    running_max, running_sum, accumulate = carried
    attended = (accumulate / running_sum[..., None]).reshape(
        local_heads, group_size, tok_rows, head_dim
    )
    attended = (
        attended.transpose(2, 0, 1, 3)
        .reshape(tok_rows, local_heads * group_size * head_dim)
        .astype(jnp.bfloat16)
    )
    summed = lax.psum_scatter(
        lax.dot_general(
            w_out, attended, (((0,), (1,)), ((), ())), preferred_element_type=jnp.float32
        ).astype(jnp.bfloat16),
        "heads",
        scatter_dimension=0,
        tiled=True,
    ).astype(jnp.float32)
    return summed.T.astype(jnp.bfloat16)


def solution(mesh):
    return jax.shard_map(
        local,
        mesh=mesh,
        in_specs=(
            P("seq", None),
            P(),
            P(None, "heads"),
            P(None, "heads"),
            P(None, "heads"),
            P("heads", None),
            P("heads", "seq", None),
            P("heads", "seq", None),
            P("heads", None),
            P("heads"),
            P("heads", None),
            P("heads"),
        ),
        out_specs=P("seq", "heads"),
        check_vma=False,
    )
```

profile of v0, /device:TPU:0, one launch (start us, length us, event | category | flops | bytes accessed | tf_op | source)
XLA Modules:
  0.0 167.0 jit_solution(1864171278540910792)
XLA Ops:
  10.1 1.4 gather_fusion
  11.5 2.0 %select_select_fusion = bf16[8,2,2,64,128]{4,3,2,0,1:T(8,128)(2,1)} fusion(bf16[8,2,2,64,128]{4,3,2,0,1:T(8,128)(2,1)} %bitcast.115, pred[8,2]{0,1:T(4,128)(4,1)S(1)} %compare_and_fusion, pred[8,2]{0,1:T(4,128)(4,1)S(1)} %bitcast.121), kind=kLoop, calls=%fused_computation.45 | loop fusion | flops 524288 | bytes 1048608 | tf_op jit(solution)/shard_map/jit(_where)/select_n | solution.py:150
  13.6 2.2 %fusion.17 = f32[256]{0:T(256)S(1)} fusion(bf16[256,4096]{1,0:T(8,128)(2,1)} %param.14), kind=kLoop, calls=%fused_computation.26 | loop fusion | flops 3145472 | bytes 2098176 | tf_op jit(solution)/shard_map/reduce_sum | solution.py:82
  15.8 3.0 %convolution_convert_fusion.2 = bf16[256,256]{1,0:T(8,128)(2,1)} fusion(bf16[4096,256]{1,0:T(8,128)(2,1)S(1)} %copy-done, bf16[256,4096]{1,0:T(8,128)(2,1)} %param.14, f32[4096]{0:T(1024)S(1)} %copy-done.7, f32[256]{0:T(256)S(1)} %add_rsqrt_fusion), kind=kOutput, calls=%fused_computation.40 | convolution fusion | flops 541130752 | bytes 4342784 | tf_op jit(solution)/shard_map/dot_general | solution.py:87
  18.8 5.7 %collective-permute-start.1 = (bf16[256,256]{1,0:T(8,128)(2,1)}, bf16[256,256]{1,0:T(8,128)(2,1)}, u32[]{:S(2)}, u32[]{:S(2)}) collective-permute-start(bf16[256,256]{1,0:T(8,128)(2,1)} %convolution_convert_fusion.2), channel_id=1, source_target_pairs={{0,1},{1,2},{2,3},{3,4},{4,5},{5,6},{6,7},{8,9},{9,10},{10,11},{11... | collective-permute-start | bytes 393224 | tf_op jit(solution)/shard_map/ppermute | solution.py:15
  25.3 3.5 %collective-permute-start = (bf16[256,256]{1,0:T(8,128)(2,1)S(1)}, bf16[256,256]{1,0:T(8,128)(2,1)}, u32[]{:S(2)}, u32[]{:S(2)}) collective-permute-start(bf16[256,256]{1,0:T(8,128)(2,1)S(1)} %convolution_convert_fusion.3), channel_id=1, source_target_pairs={{0,1},{1,2},{2,3},{3,4},{4,5},{5,6},{6,7},{8,9},{9,10},{10,11},{11... | collective-permute-start | bytes 393224 | tf_op jit(solution)/shard_map/ppermute | solution.py:15
  28.8 23.0 %all-gather = s32[8,8,2]{1,2,0:T(2,128)S(1)} all-gather(s32[1,8,2]{1,2,0:T(2,128)S(1)} %convert_bitcast_fusion), channel_id=1, replica_groups=mesh['heads'=4,'seq'=8] {'seq'}, dimensions={0}, use_global_device_ids=true | all-gather | bytes 576 | tf_op jit(solution)/shard_map/all_gather | solution.py:157
  53.0 6.9 %convolution_convert_fusion.1 = bf16[256,1024]{1,0:T(8,128)(2,1)S(1)} fusion(bf16[4096,1024]{1,0:T(8,128)(2,1)} %param.16, bf16[256,4096]{1,0:T(8,128)(2,1)} %param.14, f32[4096]{0:T(1024)S(1)} %copy-done.7, f32[256]{0:T(256)S(1)} %add_rsqrt_fusion), kind=kOutput, calls=%fused_computation.39 | convolution fusion | flops 2151940096 | bytes 11027456 | tf_op jit(solution)/shard_map/dot_general | solution.py:85
  61.6 3.7 %fusion.20 = (f32[2,1024]{1,0:T(2,128)S(1)}, f32[2,1024,512]{2,1,0:T(8,128)}) fusion(pred[2,256,512]{2,1,0:T(8,128)(4,1)S(1)} %or_and_fusion, bf16[2,1024,128]{2,1,0:T(8,128)(2,1)S(1)} %bitcast.110, bf16[256,256]{1,0:T(8,128)(2,1)S(1)} %convolution_convert_fusion.3, bf16[256,256]{1,0:T(8,128)(2,1)} %collective-permute-done), kind=kOutput, calls=%fused_computation.33 | convolution fusion | flops 272103424 | bytes 5251072 | tf_op jit(solution)/shard_map/krh,nkh->krn/dot_general | solution.py:102
  65.3 3.5 %exponential_reduce_fusion = f32[2,1024]{1,0:T(2,128)S(1)} fusion(f32[2,1024,512]{2,1,0:T(8,128)} %get-tuple-element.108, f32[2,1024]{1,0:T(2,128)S(1)} %get-tuple-element.163, pred[2,256,512]{2,1,0:T(8,128)(4,1)S(1)} %or_and_fusion), kind=kLoop, calls=%fused_computation.30 | loop fusion | flops 3143680 | bytes 4472832 | tf_op jit(solution)/shard_map/reduce_sum | solution.py:121
  68.8 2.1 %fusion.21 = f32[2,4,256,128]{3,2,1,0:T(8,128)} fusion(f32[2,4,256,512]{3,2,1,0:T(8,128)S(1)} %bitcast.112, f32[2,4,256]{2,1,0:T(4,128)S(1)} %sub.114, pred[2,256,512]{2,1,0:T(8,128)(4,1)S(1)} %or_and_fusion, bf16[512,2,128,1]{2,1,0,3:T(2,128)(2,1)S(1)} %bitcast.120), kind=kOutput, calls=%fused_computation.35 | convolution fusion | flops 271581184 | bytes 5775360 | tf_op jit(solution)/shard_map/kgtn,nkh->kgth/dot_general | solution.py:122
  70.9 22.7 %all-gather.3.cloned.1.call-done = bf16[64,2,2,64,128]{4,3,2,0,1:T(8,128)(2,1)} async-done(((bf16[8,2,2,64,128]{4,3,2,0,1:T(8,128)(2,1)}), bf16[64,2,2,64,128]{4,3,2,0,1:T(8,128)(2,1)}) %all-gather.3.cloned.1.call-update) | async-done | bytes 4194320 | tf_op jit(solution)/shard_map/all_gather | solution.py:156
  93.6 27.7 %while.14 = (s32[]{:T(128)}, f32[2,1024]{1,0:T(2,128)S(1)}, f32[2,1024]{1,0:T(2,128)S(1)}, f32[2,1024,128]{2,1,0:T(8,128)}, pred[2,32,2]{1,2,0:T(4,128)(4,1)S(1)...) while((s32[]{:T(128)}, f32[2,1024]{1,0:T(2,128)S(1)}, ...), condition=%wide.region_10.11_spmd, body=%wide.region_7.10_spmd.sunk | while | flops 2194149376 | bytes 67765592 | solution.py:55
  93.6 1.8 %copy_bitcast_fusion.2 = bf16[32,2,2,64,128]{4,3,0,1,2:T(8,128)(2,1)S(1)} fusion(bf16[2,32,2,2,64,128]{5,4,3,1,0,2:T(8,128)(2,1)} %get-tuple-element.183, s32[]{:T(128)S(6)} %copy.83), kind=kLoop, calls=%fused_computation.9.clone.1 | loop fusion | bytes 4194308 | tf_op jit(solution)/shard_map/while/body/jit(dynamic_index_in_dim)/squeeze | solution.py:55
  95.5 2.6 %bitcast_reduce_fusion.2 = (f32[2,1024]{1,0:T(2,128)S(1)}, f32[2,32,64,1024]{3,2,1,0:T(8,128)S(1)}) fusion(pred[2,32]{1,0:T(4,128)(4,1)S(1)} %dynamic-slice_bitcast_fusion.2, bf16[2,1024,128]{2,1,0:T(8,128)(2,1)S(1)} %get-tuple-element.184, bf16[32,2,2,64,128]{4,3,0,1,2:T(8,128)(2,1)S(1)} %copy_bitcast_fusion.2), kind=kOutput, calls=%fused_computation.2.clone.1 | convolution fusion | flops 1086322688 | bytes 18358784 | tf_op jit(solution)/shard_map/while/body/eval_jaxpr/krh,sknh->krsn/dot_general | solution.py:33
  98.0 3.7 %fusion.52 = f32[2,1024]{1,0:T(2,128)S(1)} fusion(f32[2,32,64,1024]{3,2,1,0:T(8,128)S(1)} %get-tuple-element.159, f32[2,1024]{1,0:T(2,128)S(1)} %max.20, pred[2,32]{1,0:T(4,128)(4,1)S(1)} %dynamic-slice_bitcast_fusion.2), kind=kLoop, calls=%fused_computation.6.clone.1 | loop fusion | flops 16775168 | bytes 16793664 | tf_op jit(solution)/shard_map/while/body/eval_jaxpr/reduce_sum | solution.py:46
  101.8 4.7 %fusion.53 = f32[2,1024,128]{2,1,0:T(8,128)S(1)} fusion(f32[2,32,64,1024]{3,2,1,0:T(8,128)S(1)} %get-tuple-element.159, f32[2,1024]{1,0:T(2,128)S(1)} %max.20, pred[2,32]{1,0:T(4,128)(4,1)S(1)} %dynamic-slice_bitcast_fusion.2, bf16[32,2,2,64,128]{4,3,0,1,2:T(8,128)(2,1)S(1)} %copy_bitcast_fusion.2, f32[2,1024,128]{2,1,0:T(8,128)S(1)} %copy-done.3, ...), kind=kOutput, calls=%fused_computation.11.clone.1 | convolution fusion | flops 1091043328 | bytes 19939840 | tf_op jit(solution)/shard_map/while/body/eval_jaxpr/krsn,sknh->krh/dot_general | solution.py:50
  107.5 1.8 %copy_bitcast_fusion.2 = bf16[32,2,2,64,128]{4,3,0,1,2:T(8,128)(2,1)S(1)} fusion(bf16[2,32,2,2,64,128]{5,4,3,1,0,2:T(8,128)(2,1)} %get-tuple-element.183, s32[]{:T(128)S(6)} %copy.83), kind=kLoop, calls=%fused_computation.9.clone.1 | loop fusion | bytes 4194308 | tf_op jit(solution)/shard_map/while/body/jit(dynamic_index_in_dim)/squeeze | solution.py:55
  109.3 2.6 %bitcast_reduce_fusion.2 = (f32[2,1024]{1,0:T(2,128)S(1)}, f32[2,32,64,1024]{3,2,1,0:T(8,128)S(1)}) fusion(pred[2,32]{1,0:T(4,128)(4,1)S(1)} %dynamic-slice_bitcast_fusion.2, bf16[2,1024,128]{2,1,0:T(8,128)(2,1)S(1)} %get-tuple-element.184, bf16[32,2,2,64,128]{4,3,0,1,2:T(8,128)(2,1)S(1)} %copy_bitcast_fusion.2), kind=kOutput, calls=%fused_computation.2.clone.1 | convolution fusion | flops 1086322688 | bytes 18358784 | tf_op jit(solution)/shard_map/while/body/eval_jaxpr/krh,sknh->krsn/dot_general | solution.py:33
  111.9 3.7 %fusion.52 = f32[2,1024]{1,0:T(2,128)S(1)} fusion(f32[2,32,64,1024]{3,2,1,0:T(8,128)S(1)} %get-tuple-element.159, f32[2,1024]{1,0:T(2,128)S(1)} %max.20, pred[2,32]{1,0:T(4,128)(4,1)S(1)} %dynamic-slice_bitcast_fusion.2), kind=kLoop, calls=%fused_computation.6.clone.1 | loop fusion | flops 16775168 | bytes 16793664 | tf_op jit(solution)/shard_map/while/body/eval_jaxpr/reduce_sum | solution.py:46
  115.6 4.7 %fusion.53 = f32[2,1024,128]{2,1,0:T(8,128)S(1)} fusion(f32[2,32,64,1024]{3,2,1,0:T(8,128)S(1)} %get-tuple-element.159, f32[2,1024]{1,0:T(2,128)S(1)} %max.20, pred[2,32]{1,0:T(4,128)(4,1)S(1)} %dynamic-slice_bitcast_fusion.2, bf16[32,2,2,64,128]{4,3,0,1,2:T(8,128)(2,1)S(1)} %copy_bitcast_fusion.2, f32[2,1024,128]{2,1,0:T(8,128)S(1)} %copy-done.3, ...), kind=kOutput, calls=%fused_computation.11.clone.1 | convolution fusion | flops 1091043328 | bytes 19939840 | tf_op jit(solution)/shard_map/while/body/eval_jaxpr/krsn,sknh->krh/dot_general | solution.py:50
  121.3 1.6 divide_convert_fusion
  123.1 7.1 %fusion.16 = bf16[4096,256]{0,1:T(8,128)(2,1)} fusion(bf16[256,1024]{0,1:T(8,128)(2,1)S(1)} %bitcast.113, bf16[1024,4096]{1,0:T(8,128)(2,1)} %param.19), kind=kOutput, calls=%fused_computation.25 | convolution fusion | flops 2148532224 | bytes 11010048 | tf_op jit(solution)/shard_map/dot_general | solution.py:171
  130.2 29.9 %reduce-scatter.2.cloned.1.call-done = bf16[1024,256]{0,1:T(8,128)(2,1)} async-done(((bf16[4096,256]{0,1:T(8,128)(2,1)}), bf16[1024,256]{0,1:T(8,128)(2,1)}) %reduce-scatter.2.cloned.1.call-update) | async-done | bytes 524304 | tf_op jit(solution)/shard_map/reduce_scatter | solution.py:170
  (65 shorter events, 9.5 us)
Async XLA Ops:
  6.5 9.3 %copy-start = (bf16[4096,256]{1,0:T(8,128)(2,1)S(1)}, bf16[4096,256]{1,0:T(8,128)(2,1)}, u32[]{:S(2)}) copy-start(bf16[4096,256]{1,0:T(8,128)(2,1)} %param.18) | copy-start | bytes 6291460
  6.5 9.3 %copy-start.7 = (f32[4096]{0:T(1024)S(1)}, f32[4096]{0:T(1024)}, u32[]{:S(2)}) copy-start(f32[4096]{0:T(1024)} %param.15) | copy-start | bytes 49156
  6.5 87.1 %all-gather.3.cloned.1.call-start = ((), (), s32[]{:S(2)}) async-start(), calls=%async_computation.1 | async-start | bytes 4718592 | tf_op jit(solution)/shard_map/all_gather | solution.py:156
  13.5 146.7 %reduce-scatter.2.cloned.1.call-start = ((), (), s32[]{:S(2)}) async-start(), calls=%async_computation.2 | async-start | bytes 2621440 | tf_op jit(solution)/shard_map/reduce_scatter | solution.py:170
  13.6 11.0 %copy-start.2 = (bf16[256,4096]{1,0:T(8,128)(2,1)S(1)}, bf16[256,4096]{1,0:T(8,128)(2,1)}, u32[]{:S(2)}) copy-start(bf16[256,4096]{1,0:T(8,128)(2,1)} %param.14) | copy-start | bytes 6291460
  13.6 10.9 %copy-start.6 = (bf16[4096,256]{1,0:T(8,128)(2,1)S(1)}, bf16[4096,256]{1,0:T(8,128)(2,1)}, u32[]{:S(2)}) copy-start(bf16[4096,256]{1,0:T(8,128)(2,1)} %param.17) | copy-start | bytes 6291460
  18.8 33.0 %copy-start.8 = (s32[2]{0:T(128)S(1)}, s32[2]{0:T(128)}, u32[]{:S(2)}) copy-start(s32[2]{0:T(128)} %param.25) | copy-start | bytes 28
  18.8 33.1 %copy-start.5 = (s32[2,4]{1,0:T(2,128)S(1)}, s32[2,4]{1,0:T(2,128)}, u32[]{:S(2)}) copy-start(s32[2,4]{1,0:T(2,128)} %param.24) | copy-start | bytes 100
  18.8 41.7 %collective-permute-start.1 = (bf16[256,256]{1,0:T(8,128)(2,1)}, bf16[256,256]{1,0:T(8,128)(2,1)}, u32[]{:S(2)}, u32[]{:S(2)}) collective-permute-start(bf16[256,256]{1,0:T(8,128)(2,1)} %convolution_convert_fusion.2), channel_id=1, source_target_pairs={{0,1},{1,2},{2,3},{3,4},{4,5},{5,6},{6,7},{8,9},{9,10},{10,11},{11... | collective-permute-start | bytes 393224 | tf_op jit(solution)/shard_map/ppermute | solution.py:15
  25.3 36.3 %collective-permute-start = (bf16[256,256]{1,0:T(8,128)(2,1)S(1)}, bf16[256,256]{1,0:T(8,128)(2,1)}, u32[]{:S(2)}, u32[]{:S(2)}) collective-permute-start(bf16[256,256]{1,0:T(8,128)(2,1)S(1)} %convolution_convert_fusion.3), channel_id=1, source_target_pairs={{0,1},{1,2},{2,3},{3,4},{4,5},{5,6},{6,7},{8,9},{9,10},{10,11},{11... | collective-permute-start | bytes 393224 | tf_op jit(solution)/shard_map/ppermute | solution.py:15
  65.3 3.5 %copy-start.1 = (f32[2,1024,512]{2,1,0:T(8,128)S(1)}, f32[2,1024,512]{2,1,0:T(8,128)}, u32[]{:S(2)}) copy-start(f32[2,1024,512]{2,1,0:T(8,128)} %get-tuple-element.108) | copy-start | bytes 12582916
  98.0 3.7 %copy-start.3 = (f32[2,1024,128]{2,1,0:T(8,128)S(1)}, f32[2,1024,128]{2,1,0:T(8,128)}, u32[]{:S(2)}) copy-start(f32[2,1024,128]{2,1,0:T(8,128)} %get-tuple-element.173) | copy-start | bytes 3145732 | tf_op jit(solution)/shard_map/while
  106.5 1.0 copy-start.4
  111.9 3.7 %copy-start.3 = (f32[2,1024,128]{2,1,0:T(8,128)S(1)}, f32[2,1024,128]{2,1,0:T(8,128)}, u32[]{:S(2)}) copy-start(f32[2,1024,128]{2,1,0:T(8,128)} %get-tuple-element.173) | copy-start | bytes 3145732 | tf_op jit(solution)/shard_map/while
  120.3 1.0 copy-start.4
Sparse Core Ops, SparseCore 0:
  13.6 79.9 all-gather.2
  130.3 29.7 reduce-scatter.1
where the time goes:
time: 167 us
  waiting for transfers between devices  52.7 us (32%)
  matrix products  38.1 us (23%)
  blocking collectives  23 us (14%)
  other arithmetic  22.4 us (13%)
  between operations  13.6 us (8%)
  starting transfers between devices  9.19 us (6%)
  local copies, waits for them, and re-layouts  7.9 us (5%)
    reduce_scatter x1, waiting for transfers between devices, local(): lax.psum_scatter(lax.dot_general(w_out, attended, (((0,), (1,)), ((), ())...  29.9 us
    all_gather x1, blocking collectives, local(): lax.all_gather(slot_live.T.astype(jnp.int32), 'seq', axis=0, tiled=True) > 0  23 us
    all_gather x1, waiting for transfers between devices, local(): lax.all_gather(kv_slots, 'seq', axis=0, tiled=True)  22.7 us
    dot_general x2, matrix products, fold_step(): jnp.einsum('krsn,sknh->krh', rounded, kv_block[:, :, 1], preferred_elemen...  9.41 us
    ppermute x2, starting transfers between devices, passed_along(): return lax.ppermute(block, axis, route)  9.14 us
    reduce_sum x2, other arithmetic, fold_step(): running_sum = running_sum * factor + jnp.sum(weights, axis=-1)  7.38 us
    dot_general x1, matrix products, local(): lax.dot_general(w_out, attended, (((0,), (1,)), ((), ())), preferred_elem...  7.11 us
    dot_general x1, matrix products, local(): jnp.dot(normed, w_query, preferred_element_type=jnp.float32)  6.94 us
  transfers between devices with their start and end apart: 4, of which 2 were waited for; matrix products, arithmetic and copies ran while one was open for 15% of the time, Pallas kernels for 0%

commit v1 on v0

v1 whole, which is shorter than its diff:
```python
import functools
import math

import jax
import jax.numpy as jnp
from jax import lax
from jax.experimental import pallas as pl
from jax.experimental.pallas import tpu as pltpu
from jax.sharding import PartitionSpec as P

BLK = 64
VCAP = 8
SMAX = 4
MESH = pl.DeviceIdType.MESH


def pick_kernel(seq, vb, vc, so, sc, ck, cv, kv, table, sems):
    heads, per_device = ck.shape[0], ck.shape[1] // BLK
    first = seq[0] * per_device
    entries = vb.shape[1]
    for i in range(table.shape[0]):
        table[i] = 0
    owners = (table.shape[0] - heads * 8) // heads
    for g in range(heads):
        for r in range(VCAP):
            table[owners * heads + g * 8 + r] = 0

        def scan(e, n):
            block = vb[g, e]
            live = (e < vc[g]) & (block >= 0)
            owner = jnp.where(live, block // per_device, 0)
            spot = g * owners + owner
            table[spot] = table[spot] + live.astype(jnp.int32)
            mine = live & (block >= first) & (block < first + per_device)

            @pl.when(mine)
            def _():
                table[owners * heads + g * 8 + n] = block - first

            return n + mine.astype(jnp.int32)

        lax.fori_loop(0, entries, scan, jnp.int32(0))
        for r in range(VCAP):
            row = pl.multiple_of(table[owners * heads + g * 8 + r] * BLK, BLK)
            for j, src in enumerate((ck, cv)):
                pltpu.make_async_copy(
                    src.at[g, pl.ds(row, BLK)],
                    kv.at[g, j, pl.ds(r * BLK, BLK)],
                    sems.at[g, j, r],
                ).start()
    for g in range(heads):
        for r in range(VCAP):
            for j, src in enumerate((ck, cv)):
                pltpu.make_async_copy(
                    src.at[g, pl.ds(0, BLK)],
                    kv.at[g, j, pl.ds(r * BLK, BLK)],
                    sems.at[g, j, r],
                ).wait()
    for g in range(heads):
        for o in range(SMAX + 1):
            hit = jnp.int32(0)
            for e in range(so.shape[1]):
                hit = hit | ((so[g, e] == o) & (e < sc[g])).astype(jnp.int32)
            table[owners * heads + g * 8 + o] = hit


def layer_kernel(
    n,
    chips,
    table,
    gain,
    tok_hbm,
    wq_hbm,
    wk_hbm,
    wv_hbm,
    wo_hbm,
    kv_hbm,
    out,
    tok,
    normed,
    wq,
    wk,
    wv,
    wo,
    kv,
    near,
    prev,
    q,
    acc,
    mx,
    sm,
    att,
    core_out,
    core_in,
    x_out,
    x_in,
    part,
    load_sem,
    own_sem,
    send_sem,
    recv_sem,
    near_send,
    near_recv,
    core_send,
    core_recv,
    x_send,
    x_recv,
):
    head = lax.axis_index("heads")
    seq = lax.axis_index("seq")
    col, row = lax.rem(seq, 2), lax.div(seq, 2)
    other = 1 - col
    length = n // 2
    groups = kv.shape[1]
    rows, hd = acc.shape[1], acc.shape[2]
    qheads = acc.shape[0]
    per = qheads // groups
    core_peer = head + 1 - 2 * lax.rem(head, 2)
    span_heads = 2 * chips

    def chip_peer(h, step):
        return lax.rem(h + 2 * step, span_heads)

    tile = wq.shape[1] // 4

    loads = [
        pltpu.make_async_copy(tok_hbm, tok, load_sem.at[0]),
        pltpu.make_async_copy(wk_hbm, wk, load_sem.at[1]),
        pltpu.make_async_copy(wv_hbm, wv, load_sem.at[2]),
    ]
    for j in range(4):
        cols = pl.ds(j * tile, tile)
        loads.append(pltpu.make_async_copy(wq_hbm.at[:, cols], wq.at[:, cols], load_sem.at[3 + j]))
    loads.append(pltpu.make_async_copy(wo_hbm, wo, load_sem.at[7]))
    own = pltpu.make_async_copy(kv_hbm, kv.at[seq], own_sem)
    own.start()
    for copy in loads:
        copy.start()

    barrier = pltpu.get_barrier_semaphore()

    def greet(h, s):
        pl.semaphore_signal(barrier, inc=1, device_id=(h, s), device_id_type=MESH)

    greet(core_peer, seq)
    for step in range(1, chips):
        greet(chip_peer(head, step), seq)
    greet(head, row * 2 + other)

    @pl.when(row > 0)
    def _():
        greet(head, seq - 2)

    @pl.when(row < length - 1)
    def _():
        greet(head, seq + 2)

    @pl.when(seq > 0)
    def _():
        greet(head, seq - 1)

    @pl.when(seq < n - 1)
    def _():
        greet(head, seq + 1)

    def flag(c):
        return jnp.where(c, 1, 0)

    pl.semaphore_wait(
        barrier,
        chips + 1 + flag(row > 0) + flag(row < length - 1) + flag(seq > 0) + flag(seq < n - 1),
    )

    def hop(s, g, way):
        target = (seq + 2, seq - 2, row * 2 + other)[way]
        return pltpu.make_async_remote_copy(
            src_ref=kv.at[s, g],
            dst_ref=kv.at[s, g],
            send_sem=send_sem.at[way, s, g],
            recv_sem=recv_sem.at[s, g],
            device_id=(head, target),
            device_id_type=MESH,
        )

    own.wait()
    for g in range(groups):

        @pl.when(row < length - 1)
        def _():
            hop(seq, g, 0).start()

        @pl.when(row > 0)
        def _():
            hop(seq, g, 1).start()

        hop(seq, g, 2).start()

    loads[0].wait()

    @pl.loop(0, rows // 32)
    def _(i):
        span = pl.ds(pl.multiple_of(i * 32, 32), 32)
        a = tok[span, :].astype(jnp.float32)
        scale = lax.rsqrt(jnp.mean(a * a, axis=-1, keepdims=True) + 1e-05)
        normed[span, :] = (a * scale * gain[...]).astype(jnp.bfloat16)

    for j, w in enumerate((wk, wv)):
        loads[1 + j].wait()
        res = jnp.dot(normed[...], w[...], preferred_element_type=jnp.float32).astype(jnp.bfloat16)
        for g in range(groups):
            near[g, j] = res[:, g * hd : (g + 1) * hd]

    for j in range(4):
        loads[3 + j].wait()
        res = jnp.dot(
            normed[...], wq[:, j * tile : (j + 1) * tile], preferred_element_type=jnp.float32
        ).astype(jnp.bfloat16)
        for k in range(tile // hd):
            q[j * (tile // hd) + k] = res[:, k * hd : (k + 1) * hd]
        if j == 0:
            shift = pltpu.make_async_remote_copy(
                src_ref=near,
                dst_ref=prev,
                send_sem=near_send,
                recv_sem=near_recv,
                device_id=(head, jnp.where(seq < n - 1, seq + 1, seq - 1)),
                device_id_type=MESH,
            )

            @pl.when(seq < n - 1)
            def _():
                shift.start()

    factor = math.log2(math.e) / math.sqrt(hd)

    def fold(h, scores, values):
        old = mx[h]
        new = jnp.maximum(old, jnp.max(scores, axis=-1, keepdims=True))
        decay = jnp.exp2((old - new) * factor)
        weights = jnp.exp2((scores - new) * factor)
        sm[h] = sm[h] * decay + jnp.sum(weights, axis=-1, keepdims=True)
        acc[h] = acc[h] * decay + jnp.dot(
            weights.astype(jnp.bfloat16), values, preferred_element_type=jnp.float32
        )
        mx[h] = new

    def similar(h, keys):
        return lax.dot_general(
            q[h], keys, (((1,), (1,)), ((), ())), preferred_element_type=jnp.float32
        )

    shape = (rows, rows)
    t_index = lax.broadcasted_iota(jnp.int32, shape, 0)
    u_index = lax.broadcasted_iota(jnp.int32, shape, 1)
    gap = t_index // BLK - u_index // BLK

    def permitted(g, offset):
        hits = jnp.zeros(shape, jnp.int32)
        for o in range(SMAX + 1):
            hits = jnp.where(gap + offset == o, table[n * groups + g * 8 + o], hits)
        return hits

    for g in range(groups):
        allowed = (permitted(g, 0) > 0) | ((gap == 0) & (u_index <= t_index))

        def first(k, _):
            h = g * per + k
            scores = jnp.where(allowed, similar(h, near[g, 0]), -jnp.inf)
            new = jnp.max(scores, axis=-1, keepdims=True)
            weights = jnp.exp2((scores - new) * factor)
            mx[h] = new
            sm[h] = jnp.sum(weights, axis=-1, keepdims=True)
            acc[h] = jnp.dot(
                weights.astype(jnp.bfloat16), near[g, 1], preferred_element_type=jnp.float32
            )
            return 0

        lax.fori_loop(0, per, first, 0)

    slots = kv.shape[3]
    slot_index = lax.broadcasted_iota(jnp.int32, (1, slots), 1)

    def attend(s, g):
        live = slot_index < table[g * n + s] * BLK

        def step(k, _):
            h = g * per + k
            fold(h, jnp.where(live, similar(h, kv[s, g, 0]), -jnp.inf), kv[s, g, 1])
            return 0

        lax.fori_loop(0, per, step, 0)

    for g in range(groups):
        attend(seq, g)

    def reach(t, d):
        r = row + t if d else row - t
        return r, (r >= 0) & (r < length)

    def rounds(t, _):
        for g in range(groups):
            for d in range(2):
                r, ok = reach(t, d)

                @pl.when(ok)
                def _():
                    s = r * 2 + col
                    hop(s, g, 2).wait_recv()

                    @pl.when((row > 0) if d else (row < length - 1))
                    def _():
                        hop(s, g, 1 if d else 0).start()

                    hop(s, g, 2).start()

            for d in range(2):
                r, ok = reach(t, d)

                @pl.when(ok)
                def _():
                    attend(r * 2 + col, g)

            for d in range(2):
                r, ok = reach(t - 1, d)
                once = ok if d else ok & (t > 1)

                @pl.when(once)
                def _():
                    s = r * 2 + other
                    hop(s, g, 2).wait_recv()
                    attend(s, g)

        @pl.when(t == 1)
        def _():
            @pl.when(seq > 0)
            def _():
                shift.wait_recv()
                for g in range(groups):
                    allowed = permitted(g, rows // BLK) > 0

                    def before(k, _):
                        h = g * per + k
                        fold(h, jnp.where(allowed, similar(h, prev[g, 0]), -jnp.inf), prev[g, 1])
                        return 0

                    lax.fori_loop(0, per, before, 0)

        return 0

    lax.fori_loop(1, length + 1, rounds, 0)

    for h in range(qheads):
        att[:, h * hd : (h + 1) * hd] = (acc[h] / sm[h]).astype(jnp.bfloat16)

    loads[7].wait()
    width = part.shape[2]
    pieces = out.shape[1] // width

    def product(target, j):
        start = pl.multiple_of(target * out.shape[1] + j * width, width)
        return jnp.dot(att[...], wo[:, pl.ds(start, width)], preferred_element_type=jnp.float32)

    def core_copy(i):
        return pltpu.make_async_remote_copy(
            src_ref=core_out.at[i],
            dst_ref=core_in.at[i],
            send_sem=core_send.at[i],
            recv_sem=core_recv.at[i],
            device_id=(core_peer, seq),
            device_id_type=MESH,
        )

    def x_copy(step, j):
        i = (step - 1) * pieces + j
        return pltpu.make_async_remote_copy(
            src_ref=x_out.at[i],
            dst_ref=x_in.at[i],
            send_sem=x_send.at[i],
            recv_sem=x_recv.at[i],
            device_id=(chip_peer(head, step), seq),
            device_id_type=MESH,
        )

    todo = [(step, j) for step in range(1, chips + 1) for j in range(pieces)]

    def exchange(i):
        step, j = todo[i]
        core_out[i] = product(chip_peer(core_peer, step), j).astype(jnp.bfloat16)
        part[i] = product(chip_peer(head, step), j)
        core_copy(i).start()

    def combine(i):
        step, j = todo[i]
        core_copy(i).wait_recv()
        both = part[i] + core_in[i].astype(jnp.float32)
        if step < chips:
            x_out[i] = both.astype(jnp.bfloat16)
        else:
            part[i] = both

    for i in range(len(todo)):
        exchange(i)
        if i > 0:
            combine(i - 1)
        if i > 1 and todo[i - 2][0] < chips:
            x_copy(*todo[i - 2]).start()
    combine(len(todo) - 1)
    if pieces == 1:
        x_copy(*todo[-2]).start()
    for j in range(pieces):
        total = part[len(todo) - pieces + j]
        for step in range(1, chips):
            x_copy(step, j).wait_recv()
            total = total + x_in[(step - 1) * pieces + j].astype(jnp.float32)
        out[:, j * width : (j + 1) * width] = total.astype(jnp.bfloat16)
    for i, (step, j) in enumerate(todo):
        core_copy(i).wait_send()
        if step < chips:
            x_copy(step, j).wait_send()

    @pl.when(seq < n - 1)
    def _():
        shift.wait_send()

    def settle(t, _):
        for g in range(groups):
            for d in range(2):
                r, ok = reach(t, d)
                once = ok if d else ok & (t > 0)

                @pl.when(once)
                def _():
                    s = r * 2 + col
                    hop(s, g, 2).wait_send()

                    @pl.when((row > 0) & ((t == 0) | (d == 1)))
                    def _():
                        hop(s, g, 1).wait_send()

                    @pl.when((row < length - 1) & ((t == 0) | (d == 0)))
                    def _():
                        hop(s, g, 0).wait_send()

        return 0

    lax.fori_loop(0, length, settle, 0)


def local(
    n,
    chips,
    tokens,
    norm_gain,
    w_query,
    w_key,
    w_value,
    w_out,
    cache_keys,
    cache_values,
    vert_blocks,
    vert_count,
    slash_offsets,
    slash_count,
):
    groups, _, hd = cache_keys.shape
    rows, model = tokens.shape
    qcols = w_query.shape[1]
    qheads = qcols // hd
    out_cols = w_out.shape[1] // (2 * chips)
    slots = VCAP * BLK
    bf16, f32 = jnp.bfloat16, jnp.float32
    smem = pl.BlockSpec(memory_space=pltpu.SMEM)
    vmem = pl.BlockSpec(memory_space=pltpu.VMEM)
    hbm = pl.BlockSpec(memory_space=pl.ANY)
    seq = lax.axis_index("seq").astype(jnp.int32).reshape(1)
    kv, table = pl.pallas_call(
        pick_kernel,
        out_shape=(
            jax.ShapeDtypeStruct((groups, 2, slots, hd), bf16),
            jax.ShapeDtypeStruct((groups * n + groups * 8,), jnp.int32),
        ),
        in_specs=[smem] * 5 + [hbm] * 2,
        out_specs=(vmem, smem),
        scratch_shapes=[pltpu.SemaphoreType.DMA((groups, 2, VCAP))],
        compiler_params=pltpu.CompilerParams(vmem_limit_bytes=4 << 20),
        name="pick",
    )(seq, vert_blocks, vert_count, slash_offsets, slash_count, cache_keys, cache_values)
    pieces = 2
    width = out_cols // pieces
    dma = pltpu.SemaphoreType.DMA
    return pl.pallas_call(
        functools.partial(layer_kernel, n, chips),
        out_shape=jax.ShapeDtypeStruct((rows, out_cols), bf16),
        in_specs=[smem, vmem] + [hbm] * 6,
        out_specs=vmem,
        scratch_shapes=[
            pltpu.VMEM((rows, model), bf16),
            pltpu.VMEM((rows, model), bf16),
            pltpu.VMEM(w_query.shape, bf16),
            pltpu.VMEM(w_key.shape, bf16),
            pltpu.VMEM(w_value.shape, bf16),
            pltpu.VMEM(w_out.shape, bf16),
            pltpu.VMEM((n, groups, 2, slots, hd), bf16),
            pltpu.VMEM((groups, 2, rows, hd), bf16),
            pltpu.VMEM((groups, 2, rows, hd), bf16),
            pltpu.VMEM((qheads, rows, hd), bf16),
            pltpu.VMEM((qheads, rows, hd), f32),
            pltpu.VMEM((qheads, rows, 1), f32),
            pltpu.VMEM((qheads, rows, 1), f32),
            pltpu.VMEM((rows, qcols), bf16),
            pltpu.VMEM((chips * pieces, rows, width), bf16),
            pltpu.VMEM((chips * pieces, rows, width), bf16),
            pltpu.VMEM(((chips - 1) * pieces, rows, width), bf16),
            pltpu.VMEM(((chips - 1) * pieces, rows, width), bf16),
            pltpu.VMEM((chips * pieces, rows, width), f32),
            dma((8,)),
            dma(()),
            dma((3, n, groups)),
            dma((n, groups)),
            dma(()),
            dma(()),
            dma((chips * pieces,)),
            dma((chips * pieces,)),
            dma(((chips - 1) * pieces,)),
            dma(((chips - 1) * pieces,)),
        ],
        compiler_params=pltpu.CompilerParams(
            collective_id=0, has_side_effects=True, vmem_limit_bytes=60 << 20
        ),
        name="layer",
    )(table, norm_gain.reshape(1, model), tokens, w_query, w_key, w_value, w_out, kv)


def solution(mesh):
    return jax.shard_map(
        functools.partial(local, mesh.shape["seq"], mesh.shape["heads"] // 2),
        mesh=mesh,
        in_specs=(
            P("seq", None),
            P(),
            P(None, "heads"),
            P(None, "heads"),
            P(None, "heads"),
            P("heads", None),
            P("heads", "seq", None),
            P("heads", "seq", None),
            P("heads", None),
            P("heads"),
            P("heads", None),
            P("heads"),
        ),
        out_specs=P("seq", "heads"),
        check_vma=False,
    )
```

time: 167 us -> 102 us (0.61)
  Pallas kernels: 0 us -> 93.8 us
  waiting for transfers between devices: 52.7 us -> 0 us
  matrix products: 38.1 us -> 0 us
  blocking collectives: 23 us -> 0 us
  other arithmetic: 22.4 us -> 0 us
  between operations: 13.6 us -> 0.03 us
  starting transfers between devices: 9.19 us -> 0 us
    pallas_call x0 -> x2, Pallas kernels: none -> 93.8 us  [the longest x1 89.2 us: local(): pl.pallas_call(functools.partial(layer_kernel, n, chips), out_shape=jax.S...]
    dot_general x10 -> x0, matrix products: 38.1 us -> none  [the longest x2 9.41 us: fold_step(): jnp.einsum('krsn,sknh->krh', rounded, kv_block[:, :, 1], preferred_elemen...]
    reduce_scatter x1 -> x0, waiting for transfers between devices: 29.9 us -> none  [local(): lax.psum_scatter(lax.dot_general(w_out, attended, (((0,), (1,)), ((), ())...]
    all_gather x1 -> x0, blocking collectives: 23 us -> none  [local(): lax.all_gather(slot_live.T.astype(jnp.int32), 'seq', axis=0, tiled=True) > 0]
    all_gather x1 -> x0, waiting for transfers between devices: 22.7 us -> none  [local(): lax.all_gather(kv_slots, 'seq', axis=0, tiled=True)]
    reduce_sum x5 -> x0, other arithmetic: 14 us -> none  [the longest x2 7.38 us: fold_step(): running_sum = running_sum * factor + jnp.sum(weights, axis=-1)]
    ppermute x2 -> x0, starting transfers between devices: 9.14 us -> none  [passed_along(): return lax.ppermute(block, axis, route)]
    unnamed x14 -> x17, local copies, waits for them, and re-layouts: 0.03 us -> 7.97 us
  transfers between devices with their start and end apart: 4 -> 0, of which waited for: 2 -> 0; matrix products, arithmetic and copies ran while one was open for 15% -> 0% of each run, Pallas kernels for 0% -> 0%
where the time goes in v1:
time: 102 us
  Pallas kernels  93.8 us (92%)
  local copies, waits for them, and re-layouts  7.97 us (8%)
    pallas_call x1, Pallas kernels, local(): pl.pallas_call(functools.partial(layer_kernel, n, chips), out_shape=jax.S...  89.2 us
    unnamed x17, local copies, waits for them, and re-layouts  7.97 us
    pallas_call x1, Pallas kernels, local(): pl.pallas_call(pick_kernel, out_shape=(jax.ShapeDtypeStruct((groups, 2, s...  4.6 us

profile of v1, /device:TPU:0, one launch (start us, length us, event | category | flops | bytes accessed | tf_op | source)
XLA Modules:
  0.0 101.8 jit_solution(9665226058015194344)
XLA Ops:
  0.0 0.0 copy-start.1
  0.0 1.0 %copy-done.1 = bf16[2,1024,128]{2,1,0:T(8,128)(2,1)S(1)} copy-done((bf16[2,1024,128]{2,1,0:T(8,128)(2,1)S(1)}, bf16[2,1024,128]{2,1,0:T(8,128)(2,1)}, u32[]{:S(2)}) %copy-start.1) | copy-done | bytes 524312
  1.0 0.0 copy-start.2
  1.0 1.0 %copy-done.2 = bf16[2,1024,128]{2,1,0:T(8,128)(2,1)S(1)} copy-done((bf16[2,1024,128]{2,1,0:T(8,128)(2,1)S(1)}, bf16[2,1024,128]{2,1,0:T(8,128)(2,1)}, u32[]{:S(2)}) %copy-start.2) | copy-done | bytes 524312
  2.1 0.0 copy-start.3
  2.1 0.7 copy-done.3
  2.8 0.0 copy-start.4
  2.8 0.7 copy-done.4
  3.4 0.0 copy-start.5
  3.4 0.7 copy-done.5
  4.1 0.0 copy-start.6
  4.1 0.7 copy-done.6
  4.8 4.6 %pick.1 = (bf16[2,2,512,128]{3,2,1,0:T(8,128)(2,1)S(1)}, s32[32]{0:T(128)S(1)}) custom-call(s32[1]{0:T(128)} %bitcast.seq, s32[2,64]{1,0:T(2,128)S(1)} %copy-done.3, s32[2]{0:T(128)S(1)} %copy-done.5, s32[2,4]{1,0:T(2,128)S(1)} %copy-done.4, s32[2]{0:T(128)S(1)} %copy-done.6, bf16[2,1024,128]{2,1,0:T(8,128)(2,1)S(1)} %copy-done.1, ...), custom_call_target="tpu_custom_call" | custom-call | tf_op jit(solution)/shard_map/pick/pallas_call | solution.py:476
  9.4 0.0 copy-start
  9.4 0.8 copy-done
  10.2 0.0 copy-start.7
  10.2 0.6 copy-done.7
  10.7 89.2 %layer.1 = bf16[256,1024]{1,0:T(8,128)(2,1)} custom-call(s32[32]{0:T(128)} %copy-done.7, f32[1,4096]{1,0:T(1,128)} %bitcast.2, bf16[256,4096]{1,0:T(8,128)(2,1)} %tok_hbm.1, bf16[4096,1024]{1,0:T(8,128)(2,1)} %wq_hbm.1, bf16[4096,256]{1,0:T(8,128)(2,1)} %wk_hbm.1, bf16[4096,256]{1,0:T(8,128)(2,1)} %wv_hbm.1, bf16[1024,4096]{1,0:T(8,128)(2,1)} %wo_hbm.1, ...), custom_call_target="tpu_custom_call" | custom-call | tf_op jit(solution)/shard_map/layer/pallas_call | solution.py:491
  99.9 1.9 %copy.14 = bf16[256,1024]{1,0:T(8,128)(2,1)} copy(bf16[256,1024]{1,0:T(8,128)(2,1)} %layer.1) | data formatting | bytes 1048576
Async XLA Ops:
  0.0 1.0 %copy-start.1 = (bf16[2,1024,128]{2,1,0:T(8,128)(2,1)S(1)}, bf16[2,1024,128]{2,1,0:T(8,128)(2,1)}, u32[]{:S(2)}) copy-start(bf16[2,1024,128]{2,1,0:T(8,128)(2,1)} %ck.1) | copy-start | bytes 1572868
  1.0 1.0 %copy-start.2 = (bf16[2,1024,128]{2,1,0:T(8,128)(2,1)S(1)}, bf16[2,1024,128]{2,1,0:T(8,128)(2,1)}, u32[]{:S(2)}) copy-start(bf16[2,1024,128]{2,1,0:T(8,128)(2,1)} %cv.1) | copy-start | bytes 1572868
  2.1 0.7 copy-start.3
  2.8 0.7 copy-start.4
  3.4 0.7 copy-start.5
  4.1 0.7 copy-start.6
  9.4 0.8 copy-start
  10.2 0.6 copy-start.7

commit v2 on v1

--- a/solution.py
+++ b/solution.py
@@ -112,9 +112,11 @@
     other = 1 - col
     length = n // 2
     groups = kv.shape[1]
-    rows, hd = acc.shape[1], acc.shape[2]
+    hd, rows = acc.shape[1], acc.shape[2]
     qheads = acc.shape[0]
     per = qheads // groups
+    mate = row + 1 - 2 * lax.rem(row, 2)
+    up = mate > row
     core_peer = head + 1 - 2 * lax.rem(head, 2)
     span_heads = 2 * chips
 
@@ -134,7 +136,7 @@
     loads.append(pltpu.make_async_copy(wo_hbm, wo, load_sem.at[7]))
     own = pltpu.make_async_copy(kv_hbm, kv.at[seq], own_sem)
     own.start()
-    for copy in loads:
+    for copy in loads[:4]:
         copy.start()
 
     barrier = pltpu.get_barrier_semaphore()
@@ -196,6 +198,8 @@
         hop(seq, g, 2).start()
 
     loads[0].wait()
+    for copy in loads[4:]:
+        copy.start()
 
     @pl.loop(0, rows // 32)
     def _(i):
@@ -231,73 +235,14 @@
             def _():
                 shift.start()
 
-    factor = math.log2(math.e) / math.sqrt(hd)
-
-    def fold(h, scores, values):
-        old = mx[h]
-        new = jnp.maximum(old, jnp.max(scores, axis=-1, keepdims=True))
-        decay = jnp.exp2((old - new) * factor)
-        weights = jnp.exp2((scores - new) * factor)
-        sm[h] = sm[h] * decay + jnp.sum(weights, axis=-1, keepdims=True)
-        acc[h] = acc[h] * decay + jnp.dot(
-            weights.astype(jnp.bfloat16), values, preferred_element_type=jnp.float32
-        )
-        mx[h] = new
-
-    def similar(h, keys):
-        return lax.dot_general(
-            q[h], keys, (((1,), (1,)), ((), ())), preferred_element_type=jnp.float32
-        )
-
-    shape = (rows, rows)
-    t_index = lax.broadcasted_iota(jnp.int32, shape, 0)
-    u_index = lax.broadcasted_iota(jnp.int32, shape, 1)
-    gap = t_index // BLK - u_index // BLK
-
-    def permitted(g, offset):
-        hits = jnp.zeros(shape, jnp.int32)
-        for o in range(SMAX + 1):
-            hits = jnp.where(gap + offset == o, table[n * groups + g * 8 + o], hits)
-        return hits
-
-    for g in range(groups):
-        allowed = (permitted(g, 0) > 0) | ((gap == 0) & (u_index <= t_index))
-
-        def first(k, _):
-            h = g * per + k
-            scores = jnp.where(allowed, similar(h, near[g, 0]), -jnp.inf)
-            new = jnp.max(scores, axis=-1, keepdims=True)
-            weights = jnp.exp2((scores - new) * factor)
-            mx[h] = new
-            sm[h] = jnp.sum(weights, axis=-1, keepdims=True)
-            acc[h] = jnp.dot(
-                weights.astype(jnp.bfloat16), near[g, 1], preferred_element_type=jnp.float32
-            )
-            return 0
-
-        lax.fori_loop(0, per, first, 0)
-
-    slots = kv.shape[3]
-    slot_index = lax.broadcasted_iota(jnp.int32, (1, slots), 1)
-
-    def attend(s, g):
-        live = slot_index < table[g * n + s] * BLK
-
-        def step(k, _):
-            h = g * per + k
-            fold(h, jnp.where(live, similar(h, kv[s, g, 0]), -jnp.inf), kv[s, g, 1])
-            return 0
-
-        lax.fori_loop(0, per, step, 0)
-
-    for g in range(groups):
-        attend(seq, g)
-
     def reach(t, d):
-        r = row + t if d else row - t
+        r = row + t * (2 * d - 1)
         return r, (r >= 0) & (r < length)
 
-    def rounds(t, _):
+    def across(r, g):
+        return (r != mate) | (g < groups - 1)
+
+    def relay(t):
         for g in range(groups):
             for d in range(2):
                 r, ok = reach(t, d)
@@ -311,46 +256,116 @@
                     def _():
                         hop(s, g, 1 if d else 0).start()
 
-                    hop(s, g, 2).start()
-
-            for d in range(2):
-                r, ok = reach(t, d)
-
-                @pl.when(ok)
-                def _():
-                    attend(r * 2 + col, g)
-
-            for d in range(2):
-                r, ok = reach(t - 1, d)
-                once = ok if d else ok & (t > 1)
-
-                @pl.when(once)
-                def _():
-                    s = r * 2 + other
+                    @pl.when(across(r, g))
+                    def _():
+                        hop(s, g, 2).start()
+
+    relay(1)
+
+    factor = math.log2(math.e) / math.sqrt(hd)
+
+    def fold(g, keys, values, allowed):
+        heads = [g * per + k for k in range(per)]
+        old = [(mx[h], sm[h], acc[h]) for h in heads]
+        fresh = []
+        for h, (m, l, a) in zip(heads, old):
+            scores = lax.dot_general(
+                keys, q[h], (((1,), (1,)), ((), ())), preferred_element_type=jnp.float32
+            )
+            scores = jnp.where(allowed, scores, -jnp.inf)
+            new = jnp.maximum(m, jnp.max(scores, axis=0, keepdims=True))
+            decay = jnp.exp2((m - new) * factor)
+            weights = jnp.exp2((scores - new) * factor)
+            l = l * decay + jnp.sum(weights, axis=0, keepdims=True)
+            a = a * decay + lax.dot_general(
+                values,
+                weights.astype(jnp.bfloat16),
+                (((0,), (0,)), ((), ())),
+                preferred_element_type=jnp.float32,
+            )
+            fresh.append((new, l, a))
+        for h, (m, l, a) in zip(heads, fresh):
+            mx[h], sm[h], acc[h] = m, l, a
+
+    shape = (rows, rows)
+    u_index = lax.broadcasted_iota(jnp.int32, shape, 0)
+    t_index = lax.broadcasted_iota(jnp.int32, shape, 1)
+    gap = t_index // BLK - u_index // BLK
+    mx[...] = jnp.full(mx.shape, -1e30, jnp.float32)
+    sm[...] = jnp.zeros(sm.shape, jnp.float32)
+    acc[...] = jnp.zeros(acc.shape, jnp.float32)
+
+    def spans(g, rows_ref, offset):
+        hits = jnp.zeros(shape, jnp.int32)
+        for o in range(SMAX + 1):
+            hits = jnp.where(gap + offset == o, table[n * groups + g * 8 + o], hits)
+        causal = (gap + offset == 0) & (u_index <= t_index)
+        fold(g, rows_ref[g, 0], rows_ref[g, 1], (hits > 0) | causal)
+        return 0
+
+    lax.fori_loop(0, groups, lambda g, _: spans(g, near, 0), 0)
+
+    slots = kv.shape[3]
+    slot_index = lax.broadcasted_iota(jnp.int32, (slots, rows), 0)
+
+    def attend(s, g):
+        fold(g, kv[s, g, 0], kv[s, g, 1], slot_index < table[g * n + s] * BLK)
+
+    def own_shard(g, _):
+        attend(seq, g)
+        return 0
+
+    lax.fori_loop(0, groups, own_shard, 0)
+
+    def visit(t, side, wait):
+        def one(i, _):
+            g, d = lax.div(i, 2), lax.rem(i, 2)
+            r, ok = reach(t, d)
+            if wait:
+                ok = ok & ((t > 0) | (d == 0)) & across(r, g)
+
+            @pl.when(ok)
+            def _():
+                s = r * 2 + side
+                if wait:
                     hop(s, g, 2).wait_recv()
-                    attend(s, g)
-
-        @pl.when(t == 1)
+                attend(s, g)
+
+            return 0
+
+        lax.fori_loop(0, 2 * groups, one, 0)
+
+    def rounds(t, _):
+        visit(t, col, False)
+
+        @pl.when(t < length - 1)
         def _():
-            @pl.when(seq > 0)
-            def _():
-                shift.wait_recv()
-                for g in range(groups):
-                    allowed = permitted(g, rows // BLK) > 0
-
-                    def before(k, _):
-                        h = g * per + k
-                        fold(h, jnp.where(allowed, similar(h, prev[g, 0]), -jnp.inf), prev[g, 1])
-                        return 0
-
-                    lax.fori_loop(0, per, before, 0)
+            relay(t + 1)
+
+        visit(t - 1, other, True)
+
+        @pl.when((t == 1) & (seq > 0))
+        def _():
+            shift.wait_recv()
+            lax.fori_loop(0, groups, lambda g, _: spans(g, prev, rows // BLK), 0)
+
+        @pl.when((t == max(length - 2, 1)) & up)
+        def _():
+            hop(row * 2 + other, groups - 1, 0).start()
+
+        @pl.when((t == max(length - 2, 1)) & jnp.logical_not(up))
+        def _():
+            hop(row * 2 + other, groups - 1, 1).start()
 
         return 0
 
     lax.fori_loop(1, length + 1, rounds, 0)
+    last = mate * 2 + other
+    hop(last, groups - 1, 2).wait_recv()
+    attend(last, groups - 1)
 
     for h in range(qheads):
-        att[:, h * hd : (h + 1) * hd] = (acc[h] / sm[h]).astype(jnp.bfloat16)
+        att[:, h * hd : (h + 1) * hd] = jnp.transpose(acc[h] / sm[h]).astype(jnp.bfloat16)
 
     loads[7].wait()
     width = part.shape[2]
@@ -431,7 +446,10 @@
                 @pl.when(once)
                 def _():
                     s = r * 2 + col
-                    hop(s, g, 2).wait_send()
+
+                    @pl.when(across(r, g))
+                    def _():
+                        hop(s, g, 2).wait_send()
 
                     @pl.when((row > 0) & ((t == 0) | (d == 1)))
                     def _():
@@ -444,6 +462,14 @@
         return 0
 
     lax.fori_loop(0, length, settle, 0)
+
+    @pl.when(up)
+    def _():
+        hop(row * 2 + other, groups - 1, 0).wait_send()
+
+    @pl.when(jnp.logical_not(up))
+    def _():
+        hop(row * 2 + other, groups - 1, 1).wait_send()
 
 
 def local(
@@ -482,7 +508,7 @@
         in_specs=[smem] * 5 + [hbm] * 2,
         out_specs=(vmem, smem),
         scratch_shapes=[pltpu.SemaphoreType.DMA((groups, 2, VCAP))],
-        compiler_params=pltpu.CompilerParams(vmem_limit_bytes=4 << 20),
+        compiler_params=pltpu.CompilerParams(vmem_limit_bytes=60 << 20),
         name="pick",
     )(seq, vert_blocks, vert_count, slash_offsets, slash_count, cache_keys, cache_values)
     pieces = 2
@@ -504,9 +530,9 @@
             pltpu.VMEM((groups, 2, rows, hd), bf16),
             pltpu.VMEM((groups, 2, rows, hd), bf16),
             pltpu.VMEM((qheads, rows, hd), bf16),
-            pltpu.VMEM((qheads, rows, hd), f32),
-            pltpu.VMEM((qheads, rows, 1), f32),
-            pltpu.VMEM((qheads, rows, 1), f32),
+            pltpu.VMEM((qheads, hd, rows), f32),
+            pltpu.VMEM((qheads, 1, rows), f32),
+            pltpu.VMEM((qheads, 1, rows), f32),
             pltpu.VMEM((rows, qcols), bf16),
             pltpu.VMEM((chips * pieces, rows, width), bf16),
             pltpu.VMEM((chips * pieces, rows, width), bf16),

time: 102 us -> 85.7 us (0.84)
  Pallas kernels: 93.8 us -> 83.1 us
  local copies, waits for them, and re-layouts: 7.97 us -> 1.87 us
    pallas_call x1, Pallas kernels: 89.2 us -> 78 us  [local(): pl.pallas_call(functools.partial(layer_kernel, n, chips), out_shape=jax.S...]
    unnamed x17 -> x1, local copies, waits for them, and re-layouts: 7.97 us -> 1.87 us
where the time goes in v2:
time: 85.7 us; the launch traced here: 85 us
  Pallas kernels  83.1 us (97%)
  local copies, waits for them, and re-layouts  1.87 us (2%)
    pallas_call x1, Pallas kernels, local(): pl.pallas_call(functools.partial(layer_kernel, n, chips), out_shape=jax.S...  78 us
    pallas_call x1, Pallas kernels, local(): pl.pallas_call(pick_kernel, out_shape=(jax.ShapeDtypeStruct((groups, 2, s...  5.07 us
    unnamed x1, local copies, waits for them, and re-layouts  1.87 us

profile of v2, /device:TPU:0, one launch (start us, length us, event | category | flops | bytes accessed | tf_op | source)
XLA Modules:
  0.0 85.0 jit_solution(14151016687577684954)
XLA Ops:
  0.0 5.1 %pick.1 = (bf16[2,2,512,128]{3,2,1,0:T(8,128)(2,1)}, s32[32]{0:T(128)}) custom-call(s32[1]{0:T(128)} %bitcast.seq, s32[2,64]{1,0:T(2,128)} %vb.1, s32[2]{0:T(128)} %vc.1, s32[2,4]{1,0:T(2,128)} %so.1, s32[2]{0:T(128)} %sc.1, bf16[2,1024,128]{2,1,0:T(8,128)(2,1)} %ck.1, bf16[2,1024,128]{2,1,0:T(8,128)(2,1)} %cv.1), custom_call_target="tpu_custom_call" | custom-call | tf_op jit(solution)/shard_map/pick/pallas_call | solution.py:502
  5.1 78.0 %layer.1 = bf16[256,1024]{1,0:T(8,128)(2,1)} custom-call(s32[32]{0:T(128)} %get-tuple-element.7.table, f32[1,4096]{1,0:T(1,128)} %bitcast.2, bf16[256,4096]{1,0:T(8,128)(2,1)} %tok_hbm.1, bf16[4096,1024]{1,0:T(8,128)(2,1)} %wq_hbm.1, bf16[4096,256]{1,0:T(8,128)(2,1)} %wk_hbm.1, bf16[4096,256]{1,0:T(8,128)(2,1)} %wv_hbm.1, bf16[1024,4096]{1,0:T(8,128)(2,1)} %wo_hbm.1, ...), custom_call_target="tpu_custom_call" | custom-call | tf_op jit(solution)/shard_map/layer/pallas_call | solution.py:517
  83.1 1.9 %copy.14 = bf16[256,1024]{1,0:T(8,128)(2,1)} copy(bf16[256,1024]{1,0:T(8,128)(2,1)} %layer.1) | data formatting | bytes 1048576
